TPU v7x, 32 devices: a whole 2x2x4 slice. The times are simulated.
32 devices in a mesh: sector: 4 (over y, x), term: 8 (over z, core).
Axes of the slice: x: 2, y: 2, z: 4, core: 2. Of those that a mesh axis runs over, the one named last changes fastest.
Arguments:
- wavefunction: float32 [4, 256, 256], P('sector'), may hold values from -6 to 6
- left_env: float32 [384, 256, 256], P(('sector', 'term')), may hold values from -0.0390625 to 0.0390625
- right_env: float32 [384, 256, 256], P(('sector', 'term')), may hold values from -0.375 to 0.375
- in_sector: int32 [384], P(('sector', 'term')), may hold values from 0 to 3
- out_sector: int32 [384], P(('sector', 'term')), may hold values from 0 to 3
- precond: float32 [4, 256, 256], P('sector'), may hold values from 2 to 4
- shifts: float32 [2], replicated, may hold values from 0.2 to 1
Outputs:
- corrected: float32 [4, 256, 256], P('sector')
- residual_norms: float32 [2], replicated
All inputs are finite; a program needn't handle non-finite values.
Results may differ from a plain program's by a relative error of at most 0.0001.
Values sent between devices are 32-bit elements; how exact they have to be, the bound alone decides.
A program may use at most 64 MiB of HBM per device.

v0:
```python
import jax
import jax.numpy as jnp
from jax import lax
from jax.sharding import PartitionSpec as P

ITERS = 2


def apply_tasks(full, left_env, right_env, in_sector, out_sector):

    def one_task(total, item):
        left, right, source, target = item
        block = lax.dynamic_index_in_dim(full, source, 0, keepdims=False)
        middle = jnp.dot(
            left, block, precision=lax.Precision.HIGHEST, preferred_element_type=jnp.float32
        )
        result = jnp.dot(
            middle, right, precision=lax.Precision.HIGHEST, preferred_element_type=jnp.float32
        )
        current = lax.dynamic_index_in_dim(total, target, 0, keepdims=False)
        total = lax.dynamic_update_index_in_dim(total, current + result, target, 0)
        return (total, None)

    start = jnp.zeros(full.shape, jnp.float32)
    total, _ = lax.scan(one_task, start, (left_env, right_env, in_sector, out_sector))
    return total


def correction(sigma, psi, precond, shift):
    residual = sigma - shift * psi
    updated = psi - residual / (precond - shift)
    return (updated, jnp.sum(residual * residual), jnp.sum(updated * updated))


def per_device(wavefunction, left_env, right_env, in_sector, out_sector, precond, shifts):
    full = lax.all_gather(wavefunction, "sector", axis=0, tiled=True)
    norms = []
    psi = wavefunction
    count = lax.axis_size("sector") * psi.size
    for step in range(ITERS):
        partial_value = apply_tasks(full, left_env, right_env, in_sector, out_sector)
        owned = lax.psum_scatter(partial_value, "sector", scatter_dimension=0, tiled=True)
        sigma = lax.psum(owned, "term")
        updated, res_sq, upd_sq = correction(sigma, psi, precond, shifts[step])
        res_total, upd_total = lax.psum((res_sq, upd_sq), "sector")
        norms.append(jnp.sqrt(res_total))
        psi = updated / jnp.sqrt(upd_total / count + 1e-06)
        if step + 1 < ITERS:
            full = lax.all_gather(psi, "sector", axis=0, tiled=True)
    return (psi, jnp.stack(norms))


def solution(mesh):
    placed = (
        P("sector", None, None),
        P(("sector", "term"), None, None),
        P(("sector", "term"), None, None),
        P(("sector", "term")),
        P(("sector", "term")),
        P("sector", None, None),
        P(),
    )
    return jax.shard_map(
        per_device,
        mesh=mesh,
        in_specs=placed,
        out_specs=(P("sector", None, None), P()),
        check_vma=False,
    )
```

profile of v0, /device:TPU:0, one launch (start us, length us, event | category | flops | bytes accessed | tf_op | source)
XLA Modules:
  0.0 478.9 jit_solution(9953802204697645868)
XLA Ops:
  7.9 31.1 %all-gather.3.cloned.1.call-done = f32[4,256,256]{2,1,0:T(8,128)} async-done(((f32[1,256,256]{2,1,0:T(8,128)}), f32[4,256,256]{2,1,0:T(8,128)}) %all-gather.3.cloned.1.call-update) | async-done | bytes 1048592 | tf_op jit(solution)/shard_map/all_gather | solution.py:36
  39.2 110.3 %while.20 = (s32[]{:T(128)}, f32[4,256,256]{2,1,0:T(8,128)S(1)}, s32[12]{0:T(128)}, f32[12,256,256]{2,1,0:T(8,128)}, s32[12]{0:T(128)}, /*index=5*/f32[4,256,256...) while((s32[]{:T(128)}, f32[4,256,256]{2,1,0:T(8,128)S(1)}, s32[12]{0:T(128)}, ...), condition=%wide.region_1.2_spmd, body=%wide.region_0.1_spmd.sunk | while | flops 402718720 | bytes 2360525 | solution.py:25
  42.4 1.4 fusion.41
  51.6 1.4 fusion.41
  60.8 1.4 fusion.41
  70.0 1.4 fusion.41
  79.2 1.4 fusion.41
  97.6 1.4 fusion.41
  116.0 1.4 fusion.41
  134.4 1.4 fusion.41
  150.6 28.0 %reduce-scatter.7.cloned.1.call-done = f32[1,256,256]{2,1,0:T(8,128)} async-done(((f32[4,256,256]{2,1,0:T(8,128)}), f32[1,256,256]{2,1,0:T(8,128)}) %reduce-scatter.7.cloned.1.call-update) | async-done | bytes 262160
  179.3 57.1 %all-reduce.6.cloned.1.call-done = f32[1,256,256]{2,1,0:T(8,128)} async-done(((f32[1,256,256]{2,1,0:T(8,128)}), f32[1,256,256]{2,1,0:T(8,128)}) %all-reduce.6.cloned.1.call-update) | async-done | bytes 262160 | tf_op jit(solution)/shard_map/psum | solution.py:43
  236.4 2.4 multiply_reduce_fusion.3
  238.8 10.4 %psum.43 = f32[]{:T(128)} all-reduce(f32[]{:T(128)} %get-tuple-element.111), channel_id=1, replica_groups=mesh['sector'=4,'term'=8] {'sector'}, use_global_device_ids=true, to_apply=%region_5.6 | all-reduce | flops 1 | bytes 8 | tf_op jit(solution)/shard_map/psum | solution.py:45
  250.7 23.8 %all-gather.5.cloned.1.call-done = f32[4,256,256]{2,1,0:T(8,128)} async-done(((f32[1,256,256]{2,1,0:T(8,128)}), f32[4,256,256]{2,1,0:T(8,128)}) %all-gather.5.cloned.1.call-update) | async-done | bytes 1048592 | tf_op jit(solution)/shard_map/all_gather | solution.py:49
  274.7 94.6 %while.21 = (s32[]{:T(128)}, f32[4,256,256]{2,1,0:T(8,128)S(1)}, s32[12]{0:T(128)S(1)}, f32[12,256,256]{2,1,0:T(8,128)}, s32[12]{0:T(128)S(1)}, /*index=5*/f32[4...) while((s32[]{:T(128)}, f32[4,256,256]{2,1,0:T(8,128)S(1)}, ...), condition=%wide.region_7.8_spmd, body=%wide.region_6.7_spmd.sunk | while | flops 402718720 | bytes 2360525 | solution.py:25
  277.2 1.4 fusion.47
  285.1 1.4 fusion.47
  293.0 1.4 fusion.47
  300.8 1.4 fusion.47
  308.7 1.4 fusion.47
  316.6 1.4 fusion.47
  324.5 1.4 fusion.47
  332.4 1.4 fusion.47
  340.2 1.4 fusion.47
  348.1 1.4 fusion.47
  356.0 1.4 fusion.47
  363.9 1.4 fusion.47
  370.3 28.0 %reduce-scatter.9.cloned.1.call-done = f32[1,256,256]{2,1,0:T(8,128)} async-done(((f32[4,256,256]{2,1,0:T(8,128)}), f32[1,256,256]{2,1,0:T(8,128)}) %reduce-scatter.9.cloned.1.call-update) | async-done | bytes 262160
  398.4 57.6 %all-reduce.8.cloned.1.call-done = f32[1,256,256]{2,1,0:T(8,128)} async-done(((f32[1,256,256]{2,1,0:T(8,128)}), f32[1,256,256]{2,1,0:T(8,128)}) %all-reduce.8.cloned.1.call-update) | async-done | bytes 262160 | tf_op jit(solution)/shard_map/psum | solution.py:43
  455.9 2.2 multiply_reduce_fusion.2
  458.2 10.5 %all-reduce.2 = (f32[]{:T(128)}, f32[]{:T(128)}, f32[]{:T(128)}) all-reduce(f32[]{:T(128)} %get-tuple-element.109, f32[]{:T(128)} %get-tuple-element.114, f32[]{:T(128)} %get-tuple-element.113), channel_id=1, replica_groups=mesh['sector'=4,'term'=8] {'sector'}, use_global_device_ids=true, to_apply=%region_11.12 | all-reduce | flops 3 | bytes 24 | tf_op jit(solution)/shard_map/psum | solution.py:45
  (132 shorter events, 88.1 us)
Async XLA Ops:
  7.2 31.9 %all-gather.3.cloned.1.call-start = ((), (), s32[]{:S(2)}) async-start(), calls=%async_computation.2 | async-start | bytes 1310720 | tf_op jit(solution)/shard_map/all_gather | solution.py:36
  7.9 170.7 %reduce-scatter.7.cloned.1.call-start = ((), (), s32[]{:S(2)}) async-start(), calls=%async_computation.6 | async-start | bytes 1310720
  39.2 139.6 %copy-start.4 = (f32[2]{0:T(128)S(1)}, f32[2]{0:T(128)}, u32[]{:S(2)}) copy-start(f32[2]{0:T(128)} %param.17) | copy-start | bytes 28
  39.2 197.2 %copy-start.2 = (f32[1,256,256]{2,1,0:T(8,128)S(1)}, f32[1,256,256]{2,1,0:T(8,128)}, u32[]{:S(2)}) copy-start(f32[1,256,256]{2,1,0:T(8,128)} %param.11) | copy-start | bytes 786436
  39.2 197.2 %copy-start.3 = (f32[1,256,256]{2,1,0:T(8,128)S(1)}, f32[1,256,256]{2,1,0:T(8,128)}, u32[]{:S(2)}) copy-start(f32[1,256,256]{2,1,0:T(8,128)} %param.16) | copy-start | bytes 786436
  149.5 1.0 copy-start.1
  149.6 125.1 %copy-start.5 = (s32[12]{0:T(128)S(1)}, s32[12]{0:T(128)}, u32[]{:S(2)}) copy-start(s32[12]{0:T(128)} %get-tuple-element.289) | copy-start | bytes 148
  149.6 125.1 %copy-start.6 = (s32[12]{0:T(128)S(1)}, s32[12]{0:T(128)}, u32[]{:S(2)}) copy-start(s32[12]{0:T(128)} %get-tuple-element.290) | copy-start | bytes 148
  150.5 85.9 %all-reduce.6.cloned.1.call-start = ((), (), s32[]{:S(2)}) async-start(), calls=%async_computation.3 | async-start | bytes 524288 | tf_op jit(solution)/shard_map/psum | solution.py:43
  178.7 95.9 %all-gather.5.cloned.1.call-start = ((), (), s32[]{:S(2)}) async-start(), calls=%async_computation.4 | async-start | bytes 1310720 | tf_op jit(solution)/shard_map/all_gather | solution.py:49
  250.7 147.7 %reduce-scatter.9.cloned.1.call-start = ((), (), s32[]{:S(2)}) async-start(), calls=%async_computation.7 | async-start | bytes 1310720
  369.2 1.0 copy-start
  370.2 85.7 %all-reduce.8.cloned.1.call-start = ((), (), s32[]{:S(2)}) async-start(), calls=%async_computation.5 | async-start | bytes 524288 | tf_op jit(solution)/shard_map/psum | solution.py:43
Sparse Core Ops, SparseCore 0:
  9.8 29.2 all-gather.2
  150.7 27.9 reduce-scatter.6
  181.0 55.4 all-reduce.5
  250.8 23.7 all-gather.4
  370.4 27.9 reduce-scatter.8
  400.5 55.4 all-reduce.7
where the time goes:
time: 482 us; the launch traced here: 479 us
  waiting for transfers between devices  226 us (47%)
  loops' own time  94.2 us (20%)
  matrix products  66.1 us (14%)
  local copies, waits for them, and re-layouts  47.3 us (10%)
  blocking collectives  20.9 us (4%)
  between operations  17 us (4%)
  other arithmetic  6.63 us (1%)
    psum x2, waiting for transfers between devices, per_device(): sigma = lax.psum(owned, 'term')  115 us
    another operation x2, loops' own time, apply_tasks(): lax.scan(one_task, start, (left_env, right_env, in_sector, out_sector))  94.2 us
    unnamed x8, waiting for transfers between devices  56.8 us
    dynamic_slice x48, local copies, waits for them, and re-layouts, apply_tasks(): lax.scan(one_task, start, (left_env, right_env, in_sector, out_sector))  44 us
    dot_general x24, matrix products, one_task(): jnp.dot(left, block, precision=lax.Precision.HIGHEST, preferred_element_t...  33.9 us
    dot_general x24, matrix products, one_task(): jnp.dot(middle, right, precision=lax.Precision.HIGHEST, preferred_element...  32.1 us
    all_gather x1, waiting for transfers between devices, per_device(): full = lax.all_gather(wavefunction, 'sector', axis=0, tiled=True)  31.1 us
    all_gather x1, waiting for transfers between devices, per_device(): full = lax.all_gather(psi, 'sector', axis=0, tiled=True)  23.8 us
  transfers between devices with their start and end apart: 6, of which 6 were waited for; matrix products, arithmetic and copies ran while one was open for 0% of the time, Pallas kernels for 0%

commit v1 on v0

--- a/solution.py
+++ b/solution.py
@@ -4,6 +4,12 @@
 from jax.sharding import PartitionSpec as P
 
 ITERS = 2
+
+
+def gather_and_add(value, name):
+    pieces = lax.all_gather(value, name, axis=0, tiled=False)
+    total = pieces.sum(axis=0)
+    return total
 
 
 def apply_tasks(full, left_env, right_env, in_sector, out_sector):
@@ -40,7 +46,7 @@
     for step in range(ITERS):
         partial_value = apply_tasks(full, left_env, right_env, in_sector, out_sector)
         owned = lax.psum_scatter(partial_value, "sector", scatter_dimension=0, tiled=True)
-        sigma = lax.psum(owned, "term")
+        sigma = gather_and_add(owned, "term")
         updated, res_sq, upd_sq = correction(sigma, psi, precond, shifts[step])
         res_total, upd_total = lax.psum((res_sq, upd_sq), "sector")
         norms.append(jnp.sqrt(res_total))

time: 482 us -> 430 us (0.89)
  waiting for transfers between devices: 226 us -> 173 us
    psum x2 -> x0, waiting for transfers between devices: 115 us -> none  [per_device(): sigma = lax.psum(owned, 'term')]
    all_gather x0 -> x2, waiting for transfers between devices: none -> 60.7 us  [gather_and_add(): pieces = lax.all_gather(value, name, axis=0, tiled=False)]
where the time goes in v1:
time: 430 us; the launch traced here: 427 us
  waiting for transfers between devices  173 us (40%)
  loops' own time  94.2 us (22%)
  matrix products  66 us (15%)
  local copies, waits for them, and re-layouts  47.2 us (11%)
  blocking collectives  21 us (5%)
  between operations  17 us (4%)
  other arithmetic  8.42 us (2%)
    another operation x2, loops' own time, apply_tasks(): lax.scan(one_task, start, (left_env, right_env, in_sector, out_sector))  94.2 us
    all_gather x2, waiting for transfers between devices, gather_and_add(): pieces = lax.all_gather(value, name, axis=0, tiled=False)  60.7 us
    unnamed x8, waiting for transfers between devices  56.8 us
    dynamic_slice x48, local copies, waits for them, and re-layouts, apply_tasks(): lax.scan(one_task, start, (left_env, right_env, in_sector, out_sector))  43.9 us
    dot_general x24, matrix products, one_task(): jnp.dot(left, block, precision=lax.Precision.HIGHEST, preferred_element_t...  33.9 us
    dot_general x24, matrix products, one_task(): jnp.dot(middle, right, precision=lax.Precision.HIGHEST, preferred_element...  32.1 us
    all_gather x1, waiting for transfers between devices, per_device(): full = lax.all_gather(wavefunction, 'sector', axis=0, tiled=True)  31.1 us
    all_gather x1, waiting for transfers between devices, per_device(): full = lax.all_gather(psi, 'sector', axis=0, tiled=True)  24.2 us
  transfers between devices with their start and end apart: 6, of which 6 were waited for; matrix products, arithmetic and copies ran while one was open for 0% of the time, Pallas kernels for 0%

profile of v1, /device:TPU:0, one launch (start us, length us, event | category | flops | bytes accessed | tf_op | source)
XLA Modules:
  0.0 426.9 jit_solution(15828881781278059368)
XLA Ops:
  7.9 31.1 %all-gather.7.cloned.1.call-done = f32[4,256,256]{2,1,0:T(8,128)} async-done(((f32[1,256,256]{2,1,0:T(8,128)}), f32[4,256,256]{2,1,0:T(8,128)}) %all-gather.7.cloned.1.call-update) | async-done | bytes 1048592 | tf_op jit(solution)/shard_map/all_gather | solution.py:42
  39.2 110.3 %while.20 = (s32[]{:T(128)}, f32[4,256,256]{2,1,0:T(8,128)S(1)}, s32[12]{0:T(128)}, f32[12,256,256]{2,1,0:T(8,128)}, s32[12]{0:T(128)}, /*index=5*/f32[4,256,256...) while((s32[]{:T(128)}, f32[4,256,256]{2,1,0:T(8,128)S(1)}, s32[12]{0:T(128)}, ...), condition=%wide.region_1.2_spmd, body=%wide.region_0.1_spmd.sunk | while | flops 402718720 | bytes 2360525 | solution.py:31
  42.4 1.4 fusion.41
  51.6 1.4 fusion.41
  60.7 1.4 fusion.41
  69.9 1.4 fusion.41
  79.1 1.4 fusion.41
  88.3 1.4 fusion.41
  97.5 1.4 fusion.41
  106.7 1.4 fusion.41
  115.9 1.4 fusion.41
  125.1 1.4 fusion.41
  134.2 1.4 fusion.41
  143.4 1.4 fusion.41
  150.5 28.0 %reduce-scatter.7.cloned.1.call-done = f32[1,256,256]{2,1,0:T(8,128)} async-done(((f32[4,256,256]{2,1,0:T(8,128)}), f32[1,256,256]{2,1,0:T(8,128)}) %reduce-scatter.7.cloned.1.call-update) | async-done | bytes 262160
  179.2 30.1 %all-gather.11.cloned.1.call-done = f32[8,256,256]{2,1,0:T(8,128)} async-done(((f32[1,256,256]{2,1,0:T(8,128)}), f32[8,256,256]{2,1,0:T(8,128)}) %all-gather.11.cloned.1.call-update) | async-done | bytes 2097168 | tf_op jit(solution)/shard_map/all_gather | solution.py:10
  209.3 1.8 reduce.2
  211.1 1.5 multiply_reduce_fusion.3
  212.5 10.4 %psum.28 = f32[]{:T(128)} all-reduce(f32[]{:T(128)} %get-tuple-element.111), channel_id=1, replica_groups=mesh['sector'=4,'term'=8] {'sector'}, use_global_device_ids=true, to_apply=%region_5.6 | all-reduce | flops 1 | bytes 8 | tf_op jit(solution)/shard_map/psum | solution.py:51
  224.5 24.2 %all-gather.9.cloned.1.call-done = f32[4,256,256]{2,1,0:T(8,128)} async-done(((f32[1,256,256]{2,1,0:T(8,128)}), f32[4,256,256]{2,1,0:T(8,128)}) %all-gather.9.cloned.1.call-update) | async-done | bytes 1048592 | tf_op jit(solution)/shard_map/all_gather | solution.py:55
  248.8 94.5 %while.21 = (s32[]{:T(128)}, f32[4,256,256]{2,1,0:T(8,128)S(1)}, s32[12]{0:T(128)S(1)}, f32[12,256,256]{2,1,0:T(8,128)}, s32[12]{0:T(128)S(1)}, /*index=5*/f32[4...) while((s32[]{:T(128)}, f32[4,256,256]{2,1,0:T(8,128)S(1)}, ...), condition=%wide.region_7.8_spmd, body=%wide.region_6.7_spmd.sunk | while | flops 402718720 | bytes 2360525 | solution.py:31
  267.1 1.4 fusion.47
  274.9 1.4 fusion.47
  290.7 1.4 fusion.47
  306.4 1.4 fusion.47
  322.2 1.4 fusion.47
  338.0 1.4 fusion.47
  344.4 28.0 %reduce-scatter.9.cloned.1.call-done = f32[1,256,256]{2,1,0:T(8,128)} async-done(((f32[4,256,256]{2,1,0:T(8,128)}), f32[1,256,256]{2,1,0:T(8,128)}) %reduce-scatter.9.cloned.1.call-update) | async-done | bytes 262160
  372.4 30.6 %all-gather.13.cloned.1.call-done = f32[8,256,256]{2,1,0:T(8,128)} async-done(((f32[1,256,256]{2,1,0:T(8,128)}), f32[8,256,256]{2,1,0:T(8,128)}) %all-gather.13.cloned.1.call-update) | async-done | bytes 2097168 | tf_op jit(solution)/shard_map/all_gather | solution.py:10
  403.0 1.8 reduce.3
  404.8 1.4 multiply_reduce_fusion.2
  406.2 10.5 %all-reduce.2 = (f32[]{:T(128)}, f32[]{:T(128)}, f32[]{:T(128)}) all-reduce(f32[]{:T(128)} %get-tuple-element.109, f32[]{:T(128)} %get-tuple-element.114, f32[]{:T(128)} %get-tuple-element.113), channel_id=1, replica_groups=mesh['sector'=4,'term'=8] {'sector'}, use_global_device_ids=true, to_apply=%region_11.12 | all-reduce | flops 3 | bytes 24 | tf_op jit(solution)/shard_map/psum | solution.py:51
  (134 shorter events, 90.8 us)
Async XLA Ops:
  7.2 31.9 %all-gather.7.cloned.1.call-start = ((), (), s32[]{:S(2)}) async-start(), calls=%async_computation.2 | async-start | bytes 1310720 | tf_op jit(solution)/shard_map/all_gather | solution.py:42
  7.9 170.6 %reduce-scatter.7.cloned.1.call-start = ((), (), s32[]{:S(2)}) async-start(), calls=%async_computation.6 | async-start | bytes 1310720
  39.2 139.4 %copy-start.4 = (f32[2]{0:T(128)S(1)}, f32[2]{0:T(128)}, u32[]{:S(2)}) copy-start(f32[2]{0:T(128)} %param.17) | copy-start | bytes 28
  149.4 1.0 copy-start
  149.4 61.6 %copy-start.2 = (f32[1,256,256]{2,1,0:T(8,128)S(1)}, f32[1,256,256]{2,1,0:T(8,128)}, u32[]{:S(2)}) copy-start(f32[1,256,256]{2,1,0:T(8,128)} %param.11) | copy-start | bytes 786436
  149.4 61.6 %copy-start.3 = (f32[1,256,256]{2,1,0:T(8,128)S(1)}, f32[1,256,256]{2,1,0:T(8,128)}, u32[]{:S(2)}) copy-start(f32[1,256,256]{2,1,0:T(8,128)} %param.16) | copy-start | bytes 786436
  149.5 99.3 %copy-start.5 = (s32[12]{0:T(128)S(1)}, s32[12]{0:T(128)}, u32[]{:S(2)}) copy-start(s32[12]{0:T(128)} %get-tuple-element.289) | copy-start | bytes 148
  149.5 99.3 %copy-start.6 = (s32[12]{0:T(128)S(1)}, s32[12]{0:T(128)}, u32[]{:S(2)}) copy-start(s32[12]{0:T(128)} %get-tuple-element.290) | copy-start | bytes 148
  150.4 58.9 %all-gather.11.cloned.1.call-start = ((), (), s32[]{:S(2)}) async-start(), calls=%async_computation.4 | async-start | bytes 2359296 | tf_op jit(solution)/shard_map/all_gather | solution.py:10
  178.5 70.1 %all-gather.9.cloned.1.call-start = ((), (), s32[]{:S(2)}) async-start(), calls=%async_computation.3 | async-start | bytes 1310720 | tf_op jit(solution)/shard_map/all_gather | solution.py:55
  224.4 148.0 %reduce-scatter.9.cloned.1.call-start = ((), (), s32[]{:S(2)}) async-start(), calls=%async_computation.7 | async-start | bytes 1310720
  343.3 1.0 copy-start.1
  344.3 58.7 %all-gather.13.cloned.1.call-start = ((), (), s32[]{:S(2)}) async-start(), calls=%async_computation.5 | async-start | bytes 2359296 | tf_op jit(solution)/shard_map/all_gather | solution.py:10
Sparse Core Ops, SparseCore 0:
  9.8 29.2 all-gather.6
  150.5 27.9 reduce-scatter.6
  180.1 29.1 all-gather.10
  224.5 24.0 all-gather.8
  344.4 27.9 reduce-scatter.8
  373.8 29.1 all-gather.12
